TPU v7x, 32 devices: a whole 2x2x4 slice. The times are simulated.
32 devices in a mesh: batch: 4 (over y, x), corpus: 8 (over z, core).
Axes of the slice: x: 2, y: 2, z: 4, core: 2. Of those that a mesh axis runs over, the one named last changes fastest.
Arguments:
- states: bfloat16 [4096, 4096], P('batch', 'corpus'), may hold values from -6 to 6
- norm_gain: float32 [4096], replicated, may hold values from 0.25 to 1.75
- gate_weight: bfloat16 [4096, 12288], P('batch', 'corpus'), may hold values from -0.09375 to 0.09375
- up_weight: bfloat16 [4096, 12288], P('batch', 'corpus'), may hold values from -0.09375 to 0.09375
- down_weight: bfloat16 [12288, 4096], P('corpus', 'batch'), may hold values from -0.0546875 to 0.0546875
- final_gain: float32 [4096], replicated, may hold values from 0.25 to 1.75
- hash_weight: bfloat16 [4096, 1024], replicated, may hold values from -0.75 to 0.75
- query_bits: bfloat16 [4096, 1024], replicated, may hold values from -1 to 1
- slot_map: int32 [64], replicated, may hold values from 0 to 63, each once
- query_index: int32 [4096, 100], replicated, may hold values from 0 to 63
Outputs:
- scores: float32 [4096, 100], P(('batch', 'corpus'))
Inputs may be any that keep to these rules, and one draw needn't show every extreme that they name: `slot_map`: each corpus entry is named by exactly one document.
All inputs are finite; a program needn't handle non-finite values.
Results may differ from a plain program's by a relative error of at most 0.017.
Values may be sent and summed in bfloat16 or wider, within the bound.
A program may use at most 192 MiB of HBM per device.

v0:
```python
import jax
import jax.numpy as jnp
from jax import lax
from jax.sharding import PartitionSpec as P

DOC_LEN = 64
CODE = 1024
NQ = 4096


def rms(values, gain):
    return values * lax.rsqrt(jnp.mean(values * values, axis=-1, keepdims=True) + 1e-06) * gain


def add_rows(left, piece):
    return jnp.dot(left, piece, preferred_element_type=jnp.float32)


def local(
    states,
    norm_gain,
    gate_weight,
    up_weight,
    down_weight,
    final_gain,
    hash_weight,
    query_bits,
    slot_map,
    query_index,
):
    corpus_count = lax.axis_size("corpus")
    devices = lax.axis_size("batch") * corpus_count
    flat_index = lax.axis_index("batch") * corpus_count + lax.axis_index("corpus")
    whole = lax.all_gather(states, "corpus", axis=1, tiled=True)
    normed = rms(whole.astype(jnp.float32), norm_gain).astype(jnp.bfloat16)

    def add_one(piece):
        return add_rows(normed, piece)

    gate = add_one(lax.all_gather(gate_weight, "batch", axis=0, tiled=True))
    up = add_one(lax.all_gather(up_weight, "batch", axis=0, tiled=True))
    hidden = (jax.nn.silu(gate) * up).astype(jnp.bfloat16)
    terms = jnp.dot(
        hidden,
        lax.all_gather(down_weight, "batch", axis=1, tiled=True),
        preferred_element_type=jnp.float32,
    )
    ffn = lax.psum_scatter(
        terms.astype(jnp.bfloat16), "corpus", scatter_dimension=0, tiled=True
    ).astype(jnp.float32)
    own_rows = ffn.shape[0]
    mine = lax.dynamic_slice_in_dim(whole, lax.axis_index("corpus") * own_rows, own_rows, 0)
    resid = mine.astype(jnp.float32) + ffn
    finals = rms(resid, final_gain)
    owned_docs = own_rows // DOC_LEN
    pooled = jnp.mean(finals.reshape(owned_docs, DOC_LEN, finals.shape[1]), axis=1).astype(
        jnp.bfloat16
    )
    codes = jnp.tanh(jnp.dot(pooled, hash_weight, preferred_element_type=jnp.float32)).astype(
        jnp.bfloat16
    )
    doc_total = owned_docs * devices
    scale = 1.0 / jnp.sqrt(jnp.float32(CODE))
    gathered = lax.all_gather(codes, ("batch", "corpus"), axis=0, tiled=True)
    placing = (slot_map[:, None] == jnp.arange(doc_total, dtype=jnp.int32)[None, :]).astype(
        jnp.bfloat16
    )
    corpus = jnp.einsum("ds,dc->sc", placing, gathered, preferred_element_type=jnp.float32).astype(
        jnp.bfloat16
    )
    query_rows = NQ // devices
    my_bits = lax.dynamic_slice_in_dim(query_bits, flat_index * query_rows, query_rows, 0)
    my_index = lax.dynamic_slice_in_dim(query_index, flat_index * query_rows, query_rows, 0)
    table = jnp.dot(my_bits, corpus.T, preferred_element_type=jnp.float32) * scale
    scores = jnp.take_along_axis(table, my_index, axis=1)
    return scores


def solution(mesh):
    placed = (
        P("batch", "corpus"),
        P(),
        P("batch", "corpus"),
        P("batch", "corpus"),
        P("corpus", "batch"),
        P(),
        P(),
        P(),
        P(),
        P(),
    )
    return jax.shard_map(
        local, mesh=mesh, in_specs=placed, out_specs=P(("batch", "corpus"), None), check_vma=False
    )
```

profile of v0, /device:TPU:0, one launch (start us, length us, event | category | flops | bytes accessed | tf_op | source)
XLA Modules:
  0.0 712.4 jit_solution(285428027022941697)
XLA Ops:
  6.5 0.0 copy-start
  6.5 0.0 all-gather.6.cloned.1.call-start
  6.5 0.7 all-gather.6.cloned.1.call-update
  7.3 0.0 copy-start.3
  7.3 0.0 all-gather.8.cloned.1.call-start
  7.3 0.7 all-gather.8.cloned.1.call-update
  8.0 0.0 all-gather.10.cloned.1.call-start
  8.1 0.7 all-gather.10.cloned.1.call-update
  8.8 0.0 all-gather.12.cloned.1.call-start
  8.8 0.5 all-gather.12.cloned.1.call-update
  9.3 0.0 reduce-scatter.2.cloned.1.call-start
  9.4 84.4 %all-gather.6.cloned.1.call-done = bf16[1024,4096]{1,0:T(8,128)(2,1)} async-done(((bf16[1024,512]{1,0:T(8,128)(2,1)}), bf16[1024,4096]{1,0:T(8,128)(2,1)}) %all-gather.6.cloned.1.call-update) | async-done | bytes 8388624 | tf_op jit(solution)/shard_map/all_gather | solution.py:34
  93.7 5.1 fusion
  98.8 117.7 %all-gather.8.cloned.1.call-done = bf16[4096,1536]{1,0:T(8,128)(2,1)} async-done(((bf16[1024,1536]{1,0:T(8,128)(2,1)}), bf16[4096,1536]{1,0:T(8,128)(2,1)}) %all-gather.8.cloned.1.call-update) | async-done | bytes 12582928 | tf_op jit(solution)/shard_map/all_gather | solution.py:40
  216.5 0.0 copy-done.3
  216.5 19.7 %fusion.4 = f32[1024,1536]{1,0:T(8,128)} fusion(bf16[4096,1536]{1,0:T(8,128)(2,1)} %all-gather.8.cloned.1.call-done, bf16[1024,4096]{1,0:T(8,128)(2,1)} %all-gather.6.cloned.1.call-done, f32[4096]{0:T(1024)S(1)} %copy-done.3, f32[1024]{0:T(1024)S(1)} %add_rsqrt_fusion), kind=kOutput, calls=%fused_computation.8 | convolution fusion | flops 12901679104 | bytes 27283456 | tf_op jit(solution)/shard_map/dot_general | solution.py:16
  236.2 104.6 %all-gather.10.cloned.1.call-done = bf16[4096,1536]{1,0:T(8,128)(2,1)} async-done(((bf16[1024,1536]{1,0:T(8,128)(2,1)}), bf16[4096,1536]{1,0:T(8,128)(2,1)}) %all-gather.10.cloned.1.call-update) | async-done | bytes 12582928 | tf_op jit(solution)/shard_map/all_gather | solution.py:41
  340.7 20.6 %multiply_convert_fusion = bf16[1024,1536]{1,0:T(8,128)(2,1)} fusion(f32[1024,1536]{1,0:T(8,128)} %fusion.4, bf16[4096,1536]{1,0:T(8,128)(2,1)} %all-gather.10.cloned.1.call-done, bf16[1024,4096]{1,0:T(8,128)(2,1)} %all-gather.6.cloned.1.call-done, f32[4096]{0:T(1024)S(1)} %copy-done.3, f32[1024]{0:T(1024)S(1)} %add_rsqrt_fusion), kind=kOutput, calls=%fused_computation.7 | convolution fusion | flops 12911116288 | bytes 30429184 | tf_op jit(solution)/shard_map/dot_general | solution.py:16
  361.4 103.5 %all-gather.12.cloned.1.call-done = bf16[1536,4096]{1,0:T(8,128)(2,1)} async-done(((bf16[1536,1024]{1,0:T(8,128)(2,1)}), bf16[1536,4096]{1,0:T(8,128)(2,1)}) %all-gather.12.cloned.1.call-update) | async-done | bytes 12582928 | tf_op jit(solution)/shard_map/all_gather | solution.py:45
  464.9 19.1 %convolution_convert_fusion = bf16[1024,4096]{1,0:T(8,128)(2,1)} fusion(bf16[1024,1536]{1,0:T(8,128)(2,1)} %multiply_convert_fusion, bf16[1536,4096]{1,0:T(8,128)(2,1)} %all-gather.12.cloned.1.call-done), kind=kOutput, calls=%fused_computation.6 | convolution fusion | flops 12889096192 | bytes 24117248 | tf_op jit(solution)/shard_map/dot_general | solution.py:43
  483.9 0.0 copy-start.1
  483.9 0.0 reduce-scatter.2.cloned.1.call-update
  483.9 0.0 copy-done
  484.0 0.1 copy.15
  484.1 0.1 reshape.33
  484.2 89.4 %reduce-scatter.2.cloned.1.call-done = bf16[128,4096]{1,0:T(8,128)(2,1)} async-done(((bf16[1024,4096]{1,0:T(8,128)(2,1)}), bf16[128,4096]{1,0:T(8,128)(2,1)}) %reduce-scatter.2.cloned.1.call-update) | async-done | bytes 1048592 | tf_op jit(solution)/shard_map/reduce_scatter | solution.py:48
  573.6 2.0 multiply_reduce_fusion
  575.6 0.0 copy-done.1
  575.6 2.0 bitcast_reduce_fusion
  577.6 0.0 copy-start.2
  577.7 4.6 fusion.9
  582.2 39.5 %all-gather = bf16[32,2,1024]{2,1,0:T(2,128)(2,1)S(1)} all-gather(bf16[1,2,1024]{2,1,0:T(2,128)(2,1)S(1)} %fusion.9), channel_id=1, replica_groups=mesh['batch'=4,'corpus'=8] {'batch','corpus'}, dimensions={0}, use_global_device_ids=true | all-gather | bytes 135168 | tf_op jit(solution)/shard_map/all_gather | solution.py:64
  621.7 0.1 reshape.45
  621.8 0.0 copy-done.2
  621.8 1.4 fusion.7
  623.2 81.8 %gather_fusion = f32[12800]{0:T(1024)S(1)} fusion(f32[128,64]{0,1:T(8,128)S(1)} %fusion.7, s32[12800]{0:T(1024)S(1)} %reshape.33), kind=kCustom, calls=%fused_computation | custom fusion | bytes 204800 | tf_op jit(solution)/shard_map/jit(take_along_axis)/gather | solution.py:75
  705.0 0.1 reshape.36
  705.2 0.7 copy.14
  (5 shorter events, 0.1 us)
Async XLA Ops:
  6.5 477.4 %copy-start = (s32[4096,100]{0,1:T(8,128)S(1)}, s32[4096,100]{0,1:T(8,128)}, u32[]{:S(2)}) copy-start(s32[4096,100]{0,1:T(8,128)} %param.19) | copy-start | bytes 4915204
  6.5 87.2 %all-gather.6.cloned.1.call-start = ((), (), s32[]{:S(2)}) async-start(), calls=%async_computation.1 | async-start | bytes 9437184 | tf_op jit(solution)/shard_map/all_gather | solution.py:34
  7.3 209.2 %copy-start.3 = (f32[4096]{0:T(1024)S(1)}, f32[4096]{0:T(1024)}, u32[]{:S(2)}) copy-start(f32[4096]{0:T(1024)} %param.11) | copy-start | bytes 49156
  7.3 209.2 %all-gather.8.cloned.1.call-start = ((), (), s32[]{:S(2)}) async-start(), calls=%async_computation.2 | async-start | bytes 15728640 | tf_op jit(solution)/shard_map/all_gather | solution.py:40
  8.0 332.7 %all-gather.10.cloned.1.call-start = ((), (), s32[]{:S(2)}) async-start(), calls=%async_computation.3 | async-start | bytes 15728640 | tf_op jit(solution)/shard_map/all_gather | solution.py:41
  8.8 456.1 %all-gather.12.cloned.1.call-start = ((), (), s32[]{:S(2)}) async-start(), calls=%async_computation.4 | async-start | bytes 15728640 | tf_op jit(solution)/shard_map/all_gather | solution.py:45
  9.3 564.3 %reduce-scatter.2.cloned.1.call-start = ((), (), s32[]{:S(2)}) async-start(), calls=%async_computation.5 | async-start | bytes 9437184 | tf_op jit(solution)/shard_map/reduce_scatter | solution.py:48
  483.9 91.7 %copy-start.1 = (f32[4096]{0:T(1024)S(1)}, f32[4096]{0:T(1024)}, u32[]{:S(2)}) copy-start(f32[4096]{0:T(1024)} %param.15) | copy-start | bytes 49156
  577.6 44.1 %copy-start.2 = (s32[64]{0:T(128)S(1)}, s32[64]{0:T(128)}, u32[]{:S(2)}) copy-start(s32[64]{0:T(128)} %param.18) | copy-start | bytes 772
Sparse Core Ops, SparseCore 0:
  8.9 84.7 all-gather.5
  95.6 120.8 all-gather.7
  218.3 122.3 all-gather.9
  342.4 122.3 all-gather.11
  484.1 89.5 reduce-scatter.1
where the time goes:
time: 713 us; the launch traced here: 712 us
  waiting for transfers between devices  502 us (70%)
  local copies, waits for them, and re-layouts  82.9 us (12%)
  matrix products  65.3 us (9%)
  blocking collectives  39.5 us (6%)
  between operations  13.3 us (2%)
  other arithmetic  9.15 us (1%)
    all_gather x1, waiting for transfers between devices, local(): gate = add_one(lax.all_gather(gate_weight, 'batch', axis=0, tiled=True))  118 us
    all_gather x1, waiting for transfers between devices, local(): up = add_one(lax.all_gather(up_weight, 'batch', axis=0, tiled=True))  105 us
    all_gather x1, waiting for transfers between devices, local(): lax.all_gather(down_weight, 'batch', axis=1, tiled=True)  103 us
    reduce_scatter x1, waiting for transfers between devices, local(): lax.psum_scatter(terms.astype(jnp.bfloat16), 'corpus', scatter_dimension=...  89.4 us
    all_gather x1, waiting for transfers between devices, local(): whole = lax.all_gather(states, 'corpus', axis=1, tiled=True)  84.4 us
    gather x3, local copies, waits for them, and re-layouts, local(): scores = jnp.take_along_axis(table, my_index, axis=1)  82 us
    dot_general x2, matrix products, add_rows(): return jnp.dot(left, piece, preferred_element_type=jnp.float32)  40.3 us
    all_gather x1, blocking collectives, local(): gathered = lax.all_gather(codes, ('batch', 'corpus'), axis=0, tiled=True)  39.5 us
  transfers between devices with their start and end apart: 5, of which 5 were waited for; matrix products, arithmetic and copies ran while one was open for 6% of the time, Pallas kernels for 0%

commit v1 on v0

--- a/solution.py
+++ b/solution.py
@@ -1,3 +1,4 @@
+import functools
 import jax
 import jax.numpy as jnp
 from jax import lax
@@ -6,6 +7,25 @@
 DOC_LEN = 64
 CODE = 1024
 NQ = 4096
+
+
+def derive_views_now(array_here, peer_axis):
+    n_all = lax.axis_size(peer_axis)
+    series = tuple(((rr, (rr + 1) % n_all) for rr in range(n_all)))
+
+    def derive_frames(arr_out):
+        if len(arr_out) == n_all:
+            return arr_out
+        return derive_frames([lax.ppermute(arr_out[0], peer_axis, perm=series), *arr_out])
+
+    return jnp.roll(
+        jnp.concatenate(derive_frames([array_here]), axis=1),
+        (lax.axis_index(peer_axis) + 1) * array_here.shape[1],
+        axis=1,
+    )
+
+
+close_the_record = functools.partial(derive_views_now, peer_axis="corpus")
 
 
 def rms(values, gain):
@@ -31,7 +51,7 @@
     corpus_count = lax.axis_size("corpus")
     devices = lax.axis_size("batch") * corpus_count
     flat_index = lax.axis_index("batch") * corpus_count + lax.axis_index("corpus")
-    whole = lax.all_gather(states, "corpus", axis=1, tiled=True)
+    whole = close_the_record(states)
     normed = rms(whole.astype(jnp.float32), norm_gain).astype(jnp.bfloat16)
 
     def add_one(piece):

time: 713 us -> 632 us (0.89)
  waiting for transfers between devices: 502 us -> 398 us
  local copies, waits for them, and re-layouts: 82.9 us -> 107 us
    all_gather x1, waiting for transfers between devices: 118 us -> 0.02 us  [local(): gate = add_one(lax.all_gather(gate_weight, 'batch', axis=0, tiled=True))]
    ppermute x0 -> x7, waiting for transfers between devices: none -> 113 us  [derive_frames(): lax.ppermute(arr_out[0], peer_axis, perm=series)]
    all_gather x1 -> x0, waiting for transfers between devices: 84.4 us -> none  [local(): whole = lax.all_gather(states, 'corpus', axis=1, tiled=True)]
    unnamed x10 -> x49, local copies, waits for them, and re-layouts: 0.16 us -> 24.5 us
    all_gather x1, waiting for transfers between devices: 105 us -> 89.4 us  [local(): up = add_one(lax.all_gather(up_weight, 'batch', axis=0, tiled=True))]
  transfers between devices with their start and end apart: 5 -> 11, of which waited for: 5 -> 10; matrix products, arithmetic and copies ran while one was open for 6% -> 9% of each run, Pallas kernels for 0% -> 0%
where the time goes in v1:
time: 632 us; the launch traced here: 631 us
  waiting for transfers between devices  398 us (63%)
  local copies, waits for them, and re-layouts  107 us (17%)
  matrix products  65.9 us (10%)
  blocking collectives  39.5 us (6%)
  between operations  13.5 us (2%)
  other arithmetic  6.46 us (1%)
    ppermute x7, waiting for transfers between devices, derive_frames(): lax.ppermute(arr_out[0], peer_axis, perm=series)  113 us
    all_gather x1, waiting for transfers between devices, local(): lax.all_gather(down_weight, 'batch', axis=1, tiled=True)  104 us
    all_gather x1, waiting for transfers between devices, local(): up = add_one(lax.all_gather(up_weight, 'batch', axis=0, tiled=True))  89.4 us
    reduce_scatter x1, waiting for transfers between devices, local(): lax.psum_scatter(terms.astype(jnp.bfloat16), 'corpus', scatter_dimension=...  89.4 us
    gather x3, local copies, waits for them, and re-layouts, local(): scores = jnp.take_along_axis(table, my_index, axis=1)  82 us
    dot_general x2, matrix products, add_rows(): return jnp.dot(left, piece, preferred_element_type=jnp.float32)  40.8 us
    all_gather x1, blocking collectives, local(): gathered = lax.all_gather(codes, ('batch', 'corpus'), axis=0, tiled=True)  39.5 us
    unnamed x49, local copies, waits for them, and re-layouts  24.5 us
  transfers between devices with their start and end apart: 11, of which 10 were waited for; matrix products, arithmetic and copies ran while one was open for 9% of the time, Pallas kernels for 0%

profile of v1, /device:TPU:0, one launch (start us, length us, event | category | flops | bytes accessed | tf_op | source)
XLA Modules:
  0.0 631.2 jit_solution(8917958217705613876)
XLA Ops:
  6.5 0.7 all-gather.5.cloned.1.call-update
  7.3 0.0 all-gather.7.cloned.1.call-start
  7.3 0.7 all-gather.7.cloned.1.call-update
  8.0 0.0 all-gather.9.cloned.1.call-start
  8.1 0.7 all-gather.9.cloned.1.call-update
  8.7 0.0 reduce-scatter.2.cloned.1.call-start
  8.8 0.5 collective-permute-start
  9.3 16.7 %collective-permute-done = bf16[1024,512]{1,0:T(8,128)(2,1)S(1)} collective-permute-done((bf16[1024,512]{1,0:T(8,128)(2,1)}, bf16[1024,512]{1,0:T(8,128)(2,1)S(1)}, u32[]{:S(2)}, u32[]{:S(2)}) %collective-permute-start) | collective-permute-done | bytes 1048608 | tf_op jit(solution)/shard_map/ppermute | solution.py:19
  26.1 1.0 copy-done.3
  27.0 0.0 collective-permute-start.1
  27.0 16.0 %collective-permute-done.1 = bf16[1024,512]{1,0:T(8,128)(2,1)S(1)} collective-permute-done((bf16[1024,512]{1,0:T(8,128)(2,1)S(1)}, bf16[1024,512]{1,0:T(8,128)(2,1)S(1)}, u32[]{:S(2)}, u32[]{:S(2)}) %collective-permute-start.1) | collective-permute-done | bytes 1048608 | tf_op jit(solution)/shard_map/ppermute | solution.py:19
  43.0 1.0 copy-done.5
  44.0 0.0 collective-permute-start.2
  44.0 16.0 %collective-permute-done.2 = bf16[1024,512]{1,0:T(8,128)(2,1)S(1)} collective-permute-done((bf16[1024,512]{1,0:T(8,128)(2,1)S(1)}, bf16[1024,512]{1,0:T(8,128)(2,1)S(1)}, u32[]{:S(2)}, u32[]{:S(2)}) %collective-permute-start.2) | collective-permute-done | bytes 1048608 | tf_op jit(solution)/shard_map/ppermute | solution.py:19
  60.1 1.0 copy-done.7
  61.0 0.0 collective-permute-start.3
  61.0 16.0 %collective-permute-done.3 = bf16[1024,512]{1,0:T(8,128)(2,1)S(1)} collective-permute-done((bf16[1024,512]{1,0:T(8,128)(2,1)S(1)}, bf16[1024,512]{1,0:T(8,128)(2,1)S(1)}, u32[]{:S(2)}, u32[]{:S(2)}) %collective-permute-start.3) | collective-permute-done | bytes 1048608 | tf_op jit(solution)/shard_map/ppermute | solution.py:19
  77.0 1.0 copy-done.9
  78.0 0.0 collective-permute-start.4
  78.0 16.0 %collective-permute-done.4 = bf16[1024,512]{1,0:T(8,128)(2,1)S(1)} collective-permute-done((bf16[1024,512]{1,0:T(8,128)(2,1)S(1)}, bf16[1024,512]{1,0:T(8,128)(2,1)S(1)}, u32[]{:S(2)}, u32[]{:S(2)}) %collective-permute-start.4) | collective-permute-done | bytes 1048608 | tf_op jit(solution)/shard_map/ppermute | solution.py:19
  94.1 1.0 copy-done.11
  95.0 0.0 collective-permute-start.5
  95.0 16.1 %collective-permute-done.5 = bf16[1024,512]{1,0:T(8,128)(2,1)} collective-permute-done((bf16[1024,512]{1,0:T(8,128)(2,1)S(1)}, bf16[1024,512]{1,0:T(8,128)(2,1)}, u32[]{:S(2)}, u32[]{:S(2)}) %collective-permute-start.5) | collective-permute-done | bytes 1048608 | tf_op jit(solution)/shard_map/ppermute | solution.py:19
  111.2 0.0 collective-permute-start.6
  111.2 16.3 %collective-permute-done.6 = bf16[1024,512]{1,0:T(8,128)(2,1)} collective-permute-done((bf16[1024,512]{1,0:T(8,128)(2,1)}, bf16[1024,512]{1,0:T(8,128)(2,1)}, u32[]{:S(2)}, u32[]{:S(2)}) %collective-permute-start.6) | collective-permute-done | bytes 1048608 | tf_op jit(solution)/shard_map/ppermute | solution.py:19
  127.5 1.3 constant_dynamic-update-slice_fusion.15
  128.9 0.0 copy-start.6
  128.9 1.4 constant_dynamic-update-slice_fusion.14
  130.3 1.3 constant_dynamic-update-slice_fusion.13
  131.7 1.3 constant_dynamic-update-slice_fusion.12
  133.0 1.3 constant_dynamic-update-slice_fusion.11
  134.4 1.3 constant_dynamic-update-slice_fusion.10
  135.7 0.1 constant_dynamic-update-slice_fusion.9
  135.9 0.1 constant_dynamic-update-slice_fusion.8
  136.0 0.0 copy-start.15
  136.0 1.4 constant_dynamic-update-slice_fusion.7
  137.4 1.3 constant_dynamic-update-slice_fusion.6
  138.7 0.1 constant_dynamic-update-slice_fusion.5
  138.9 0.1 constant_dynamic-update-slice_fusion.4
  139.0 0.1 constant_dynamic-update-slice_fusion.3
  139.2 0.1 constant_dynamic-update-slice_fusion.2
  139.3 0.1 constant_dynamic-update-slice_fusion.1
  139.4 0.1 constant_dynamic-update-slice_fusion
  139.6 7.7 %copy-done.1 = bf16[1024,8192]{1,0:T(8,128)(2,1)} copy-done((bf16[1024,8192]{1,0:T(8,128)(2,1)}, bf16[1024,8192]{1,0:T(8,128)(2,1)S(1)}, u32[]{:S(2)}) %copy-start.1) | copy-done | bytes 16777240
  147.3 1.7 fusion
  149.0 0.0 all-gather.5.cloned.1.call-done
  149.1 20.1 %fusion.4 = f32[1024,1536]{1,0:T(8,128)} fusion(bf16[4096,1536]{1,0:T(8,128)(2,1)} %all-gather.5.cloned.1.call-done, f32[4096]{0:T(1024)S(1)} %copy-done.15, f32[1024]{0:T(1024)S(1)} %add_rsqrt_fusion, bf16[1024,8192]{1,0:T(8,128)(2,1)} %copy-done.1, s32[]{:T(128)S(6)} %select_n.37), kind=kOutput, calls=%fused_computation.12 | convolution fusion | flops 12901679104 | bytes 27283460 | tf_op jit(solution)/shard_map/dot_general | solution.py:36
  169.1 89.4 %all-gather.7.cloned.1.call-done = bf16[4096,1536]{1,0:T(8,128)(2,1)} async-done(((bf16[1024,1536]{1,0:T(8,128)(2,1)}), bf16[4096,1536]{1,0:T(8,128)(2,1)}) %all-gather.7.cloned.1.call-update) | async-done | bytes 12582928 | tf_op jit(solution)/shard_map/all_gather | solution.py:61
  258.6 20.7 %multiply_convert_fusion = bf16[1024,1536]{1,0:T(8,128)(2,1)} fusion(f32[1024,1536]{1,0:T(8,128)} %fusion.4, bf16[4096,1536]{1,0:T(8,128)(2,1)} %all-gather.7.cloned.1.call-done, f32[4096]{0:T(1024)S(1)} %copy-done.15, f32[1024]{0:T(1024)S(1)} %add_rsqrt_fusion, bf16[1024,8192]{1,0:T(8,128)(2,1)} %copy-done.1, s32[]{:T(128)S(6)} %select_n.37), kind=kOutput, calls=%fused_computation.7 | convolution fusion | flops 12911116288 | bytes 30429188 | tf_op jit(solution)/shard_map/dot_general | solution.py:36
  279.2 103.6 %all-gather.9.cloned.1.call-done = bf16[1536,4096]{1,0:T(8,128)(2,1)} async-done(((bf16[1536,1024]{1,0:T(8,128)(2,1)}), bf16[1536,4096]{1,0:T(8,128)(2,1)}) %all-gather.9.cloned.1.call-update) | async-done | bytes 12582928 | tf_op jit(solution)/shard_map/all_gather | solution.py:65
  382.8 19.1 %convolution_convert_fusion = bf16[1024,4096]{1,0:T(8,128)(2,1)} fusion(bf16[1024,1536]{1,0:T(8,128)(2,1)} %multiply_convert_fusion, bf16[1536,4096]{1,0:T(8,128)(2,1)} %all-gather.9.cloned.1.call-done), kind=kOutput, calls=%fused_computation.6 | convolution fusion | flops 12889096192 | bytes 24117248 | tf_op jit(solution)/shard_map/dot_general | solution.py:63
  401.9 0.0 reduce-scatter.2.cloned.1.call-update
  402.0 0.1 copy.15
  402.2 0.1 reshape.33
  402.3 89.4 %reduce-scatter.2.cloned.1.call-done = bf16[128,4096]{1,0:T(8,128)(2,1)} async-done(((bf16[1024,4096]{1,0:T(8,128)(2,1)}), bf16[128,4096]{1,0:T(8,128)(2,1)}) %reduce-scatter.2.cloned.1.call-update) | async-done | bytes 1048592 | tf_op jit(solution)/shard_map/reduce_scatter | solution.py:68
  491.6 2.3 multiply_reduce_fusion
  494.0 2.4 bitcast_reduce_fusion
  496.4 4.6 fusion.9
  501.0 39.5 %all-gather = bf16[32,2,1024]{2,1,0:T(2,128)(2,1)S(1)} all-gather(bf16[1,2,1024]{2,1,0:T(2,128)(2,1)S(1)} %fusion.9), channel_id=1, replica_groups=mesh['batch'=4,'corpus'=8] {'batch','corpus'}, dimensions={0}, use_global_device_ids=true | all-gather | bytes 135168 | tf_op jit(solution)/shard_map/all_gather | solution.py:84
  540.5 0.1 reshape.45
  540.5 1.4 fusion.7
  541.9 81.8 %gather_fusion = f32[12800]{0:T(1024)S(1)} fusion(f32[128,64]{0,1:T(8,128)S(1)} %fusion.7, s32[12800]{0:T(1024)S(1)} %reshape.33), kind=kCustom, calls=%fused_computation | custom fusion | bytes 204800 | tf_op jit(solution)/shard_map/jit(take_along_axis)/gather | solution.py:95
  623.7 0.1 reshape.36
  623.9 0.7 copy.14
  (30 shorter events, 0.1 us)
Async XLA Ops:
  6.5 395.4 %copy-start = (s32[4096,100]{0,1:T(8,128)S(1)}, s32[4096,100]{0,1:T(8,128)}, u32[]{:S(2)}) copy-start(s32[4096,100]{0,1:T(8,128)} %param.19) | copy-start | bytes 4915204
  6.5 129.3 %copy-start.2 = (bf16[1024,512]{1,0:T(8,128)(2,1)S(1)}, bf16[1024,512]{1,0:T(8,128)(2,1)}, u32[]{:S(2)}) copy-start(bf16[1024,512]{1,0:T(8,128)(2,1)} %param.10) | copy-start | bytes 3145732
  6.5 142.5 %all-gather.5.cloned.1.call-start = ((), (), s32[]{:S(2)}) async-start(), calls=%async_computation.1 | async-start | bytes 15728640 | tf_op jit(solution)/shard_map/all_gather | solution.py:60
  7.3 251.3 %all-gather.7.cloned.1.call-start = ((), (), s32[]{:S(2)}) async-start(), calls=%async_computation.2 | async-start | bytes 15728640 | tf_op jit(solution)/shard_map/all_gather | solution.py:61
  8.0 374.8 %all-gather.9.cloned.1.call-start = ((), (), s32[]{:S(2)}) async-start(), calls=%async_computation.3 | async-start | bytes 15728640 | tf_op jit(solution)/shard_map/all_gather | solution.py:65
  8.7 482.9 %reduce-scatter.2.cloned.1.call-start = ((), (), s32[]{:S(2)}) async-start(), calls=%async_computation.4 | async-start | bytes 9437184 | tf_op jit(solution)/shard_map/reduce_scatter | solution.py:68
  8.8 17.3 %collective-permute-start = (bf16[1024,512]{1,0:T(8,128)(2,1)}, bf16[1024,512]{1,0:T(8,128)(2,1)S(1)}, u32[]{:S(2)}, u32[]{:S(2)}) collective-permute-start(bf16[1024,512]{1,0:T(8,128)(2,1)} %param.10), channel_id=1, source_target_pairs={{0,1},{1,2},{2,3},{3,4},{4,5},{5,6},{6,7},{7,0},{8,9},{9,10},{10,1... | collective-permute-start | bytes 3145736 | tf_op jit(solution)/shard_map/ppermute | solution.py:19
  26.1 1.0 copy-start.3
  27.0 16.0 %collective-permute-start.1 = (bf16[1024,512]{1,0:T(8,128)(2,1)S(1)}, bf16[1024,512]{1,0:T(8,128)(2,1)S(1)}, u32[]{:S(2)}, u32[]{:S(2)}) collective-permute-start(bf16[1024,512]{1,0:T(8,128)(2,1)S(1)} %collective-permute-done), channel_id=1, source_target_pairs={{0,1},{1,2},{2,3},{3,4},{4,5},{5,6},{6,7},{7,0},{8,9},{9,10},{10,1... | collective-permute-start | bytes 3145736 | tf_op jit(solution)/shard_map/ppermute | solution.py:19
  43.0 1.0 copy-start.5
  44.0 16.0 %collective-permute-start.2 = (bf16[1024,512]{1,0:T(8,128)(2,1)S(1)}, bf16[1024,512]{1,0:T(8,128)(2,1)S(1)}, u32[]{:S(2)}, u32[]{:S(2)}) collective-permute-start(bf16[1024,512]{1,0:T(8,128)(2,1)S(1)} %collective-permute-done.1), channel_id=1, source_target_pairs={{0,1},{1,2},{2,3},{3,4},{4,5},{5,6},{6,7},{7,0},{8,9},{9,10},{10,1... | collective-permute-start | bytes 3145736 | tf_op jit(solution)/shard_map/ppermute | solution.py:19
  60.1 1.0 copy-start.7
  61.0 16.0 %collective-permute-start.3 = (bf16[1024,512]{1,0:T(8,128)(2,1)S(1)}, bf16[1024,512]{1,0:T(8,128)(2,1)S(1)}, u32[]{:S(2)}, u32[]{:S(2)}) collective-permute-start(bf16[1024,512]{1,0:T(8,128)(2,1)S(1)} %collective-permute-done.2), channel_id=1, source_target_pairs={{0,1},{1,2},{2,3},{3,4},{4,5},{5,6},{6,7},{7,0},{8,9},{9,10},{10,1... | collective-permute-start | bytes 3145736 | tf_op jit(solution)/shard_map/ppermute | solution.py:19
  77.0 1.0 copy-start.9
  78.0 16.0 %collective-permute-start.4 = (bf16[1024,512]{1,0:T(8,128)(2,1)S(1)}, bf16[1024,512]{1,0:T(8,128)(2,1)S(1)}, u32[]{:S(2)}, u32[]{:S(2)}) collective-permute-start(bf16[1024,512]{1,0:T(8,128)(2,1)S(1)} %collective-permute-done.3), channel_id=1, source_target_pairs={{0,1},{1,2},{2,3},{3,4},{4,5},{5,6},{6,7},{7,0},{8,9},{9,10},{10,1... | collective-permute-start | bytes 3145736 | tf_op jit(solution)/shard_map/ppermute | solution.py:19
  94.1 1.0 copy-start.11
  95.0 16.1 %collective-permute-start.5 = (bf16[1024,512]{1,0:T(8,128)(2,1)S(1)}, bf16[1024,512]{1,0:T(8,128)(2,1)}, u32[]{:S(2)}, u32[]{:S(2)}) collective-permute-start(bf16[1024,512]{1,0:T(8,128)(2,1)S(1)} %collective-permute-done.4), channel_id=1, source_target_pairs={{0,1},{1,2},{2,3},{3,4},{4,5},{5,6},{6,7},{7,0},{8,9},{9,10},{10,1... | collective-permute-start | bytes 3145736 | tf_op jit(solution)/shard_map/ppermute | solution.py:19
  111.2 16.3 %collective-permute-start.6 = (bf16[1024,512]{1,0:T(8,128)(2,1)}, bf16[1024,512]{1,0:T(8,128)(2,1)}, u32[]{:S(2)}, u32[]{:S(2)}) collective-permute-start(bf16[1024,512]{1,0:T(8,128)(2,1)} %collective-permute-done.5), channel_id=1, source_target_pairs={{0,1},{1,2},{2,3},{3,4},{4,5},{5,6},{6,7},{7,0},{8,9},{9,10},{10,1... | collective-permute-start | bytes 3145736 | tf_op jit(solution)/shard_map/ppermute | solution.py:19
  111.2 24.6 %copy-start.4 = (bf16[1024,512]{1,0:T(8,128)(2,1)S(1)}, bf16[1024,512]{1,0:T(8,128)(2,1)}, u32[]{:S(2)}) copy-start(bf16[1024,512]{1,0:T(8,128)(2,1)} %copy-done.3) | copy-start | bytes 3145732
  111.2 27.6 %copy-start.12 = (bf16[1024,512]{1,0:T(8,128)(2,1)S(1)}, bf16[1024,512]{1,0:T(8,128)(2,1)}, u32[]{:S(2)}) copy-start(bf16[1024,512]{1,0:T(8,128)(2,1)} %copy-done.11) | copy-start | bytes 3145732
  111.2 27.7 %copy-start.10 = (bf16[1024,512]{1,0:T(8,128)(2,1)S(1)}, bf16[1024,512]{1,0:T(8,128)(2,1)}, u32[]{:S(2)}) copy-start(bf16[1024,512]{1,0:T(8,128)(2,1)} %copy-done.9) | copy-start | bytes 3145732
  111.2 27.8 %copy-start.8 = (bf16[1024,512]{1,0:T(8,128)(2,1)S(1)}, bf16[1024,512]{1,0:T(8,128)(2,1)}, u32[]{:S(2)}) copy-start(bf16[1024,512]{1,0:T(8,128)(2,1)} %copy-done.7) | copy-start | bytes 3145732
  128.9 10.3 %copy-start.6 = (bf16[1024,512]{1,0:T(8,128)(2,1)S(1)}, bf16[1024,512]{1,0:T(8,128)(2,1)}, u32[]{:S(2)}) copy-start(bf16[1024,512]{1,0:T(8,128)(2,1)} %copy-done.5) | copy-start | bytes 3145732
  136.0 13.0 %copy-start.15 = (f32[4096]{0:T(1024)S(1)}, f32[4096]{0:T(1024)}, u32[]{:S(2)}) copy-start(f32[4096]{0:T(1024)} %param.11) | copy-start | bytes 49156
  139.6 7.8 %copy-start.1 = (bf16[1024,8192]{1,0:T(8,128)(2,1)}, bf16[1024,8192]{1,0:T(8,128)(2,1)S(1)}, u32[]{:S(2)}) copy-start(bf16[1024,8192]{1,0:T(8,128)(2,1)S(1)} %constant_dynamic-update-slice_fusion) | copy-start | bytes 50331652
  279.2 214.7 %copy-start.13 = (f32[4096]{0:T(1024)S(1)}, f32[4096]{0:T(1024)}, u32[]{:S(2)}) copy-start(f32[4096]{0:T(1024)} %param.15) | copy-start | bytes 49156
  401.9 138.6 %copy-start.14 = (s32[64]{0:T(128)S(1)}, s32[64]{0:T(128)}, u32[]{:S(2)}) copy-start(s32[64]{0:T(128)} %param.18) | copy-start | bytes 772
Sparse Core Ops, SparseCore 0:
  9.2 125.0 all-gather.4
  136.2 122.3 all-gather.6
  260.4 122.3 all-gather.8
  402.1 89.5 reduce-scatter.1
